TPU v7x, 512 devices: a whole 4x8x8 slice. The times are simulated.
512 devices in a mesh: dp: 8 (over y), seq: 64 (over z, x, core).
Axes of the slice: x: 4, y: 8, z: 8, core: 2. Of those that a mesh axis runs over, the one named last changes fastest.
Arguments:
- mel_frames: bfloat16 [8, 16384, 128], P('dp', 'seq'), may hold values from -16 to 16
- positions: int32 [8, 8192], P('dp', 'seq'), may hold values from 0 to 16383, as said below
- conv_weight: bfloat16 [128, 3, 1280], replicated, may hold values from -0.3125 to 0.3125
- conv_bias: float32 [1280], replicated, may hold values from -3 to 3
- proj_weight: bfloat16 [1280, 2048], P('dp'), may hold values from -0.15625 to 0.15625
- proj_bias: float32 [2048], replicated, may hold values from -3 to 3
- cotangent: bfloat16 [8, 16384, 2048], P('dp', 'seq'), may hold values from -0.032958984 to 0.032958984
Outputs:
- merged: bfloat16 [8, 16384, 2048], P('dp', 'seq')
- grad_weight: float32 [128, 3, 1280], P('seq', None, 'dp')
Inputs may be any that keep to these rules, and one draw needn't show every extreme that they name: Within a recording the 8192 entries are distinct. Block b of the sequence is positions b * 256 to b * 256 + 255; the 128 tokens of one window put at most 4 entries into any one block, and in each recording one block receives exactly 4 from every window.
All inputs are finite; a program needn't handle non-finite values.
Results may differ from a plain program's by a relative error of at most 0.012.
Values may be sent and summed in bfloat16 or wider, within the bound.
A program may use at most 64 MiB of HBM per device.

v0:
```python
import jax
import jax.numpy as jnp
from jax import lax
from jax.sharding import PartitionSpec as P

SQRT_HALF = 0.7071067811865476
INV_SQRT_TWO_PI = 0.3989422804014327


def gelu_value(x):
    return x * 0.5 * (1.0 + lax.erf(x * SQRT_HALF))


def gelu_slope(x):
    return 0.5 * (1.0 + lax.erf(x * SQRT_HALF)) + x * INV_SQRT_TWO_PI * jnp.exp(-0.5 * x * x)


def body(mel_frames, positions, conv_weight, conv_bias, proj_weight, proj_bias, cotangent):
    frames = mel_frames[0]
    local_spots = positions[0]
    grads_in = cotangent[0]
    owner_count = lax.axis_size("seq")
    frame_count = frames.shape[0]
    tok_count = frame_count // 2
    rows_own = grads_in.shape[0]
    capacity = rows_own // owner_count
    tap_count = conv_weight.shape[1]
    channels = conv_weight.shape[2]
    padded = jnp.pad(frames, ((1, 1), (0, 0)))
    stacked = jnp.concatenate([padded[k : k + frame_count] for k in range(tap_count)], axis=1)
    kernel = jnp.transpose(conv_weight, (1, 0, 2)).reshape(-1, channels)
    pre_act = jnp.dot(stacked, kernel, preferred_element_type=jnp.float32) + conv_bias
    act_pairs = gelu_value(pre_act).reshape(tok_count, 2, channels)
    pooled = (0.5 * (act_pairs[:, 0, :] + act_pairs[:, 1, :])).astype(jnp.bfloat16)
    full_weight = lax.all_gather(proj_weight, "dp", axis=0, tiled=True)
    owner_index = local_spots // rows_own
    owner_row = local_spots % rows_own
    onehot = (owner_index[:, None] == jnp.arange(owner_count, dtype=jnp.int32)[None, :]).astype(
        jnp.int32
    )
    rank_before = jnp.cumsum(onehot, axis=0) - onehot
    slot_rank = jnp.sum(rank_before * onehot, axis=1)
    slot_index = owner_index * capacity + slot_rank
    dest_rows = (
        jnp.full((owner_count * capacity,), rows_own, jnp.int32).at[slot_index].set(owner_row)
    )
    dest_rows = dest_rows.reshape(owner_count, capacity)
    contract_last = (((1,), (1,)), ((), ()))
    projected = (
        jnp.dot(pooled, full_weight, preferred_element_type=jnp.float32) + proj_bias
    ).astype(jnp.bfloat16)
    outgoing = (
        jnp.zeros((owner_count * capacity, projected.shape[1]), jnp.bfloat16)
        .at[slot_index]
        .set(projected)
    )
    outgoing = outgoing.reshape(owner_count, capacity, -1)
    arrived, arrived_rows = (
        lax.all_to_all(outgoing, "seq", split_axis=0, concat_axis=0, tiled=True),
        lax.all_to_all(dest_rows, "seq", split_axis=0, concat_axis=0, tiled=True),
    )
    flat_rows = arrived_rows.reshape(-1)
    merged = (
        jnp.zeros_like(grads_in)
        .at[flat_rows]
        .set(arrived.reshape(flat_rows.shape[0], -1), mode="drop")
    )
    picked = jnp.take(grads_in, flat_rows, axis=0, mode="clip").reshape(owner_count, capacity, -1)
    returned = lax.all_to_all(picked, "seq", split_axis=0, concat_axis=0, tiled=True)
    grad_tokens = returned.reshape(owner_count * capacity, -1)[slot_index]
    grad_pooled = lax.dot_general(
        grad_tokens, full_weight, contract_last, preferred_element_type=jnp.float32
    ).astype(jnp.bfloat16)
    slopes = gelu_slope(pre_act).reshape(tok_count, 2, channels)
    grad_pre = (0.5 * grad_pooled.astype(jnp.float32)[:, None, :] * slopes).astype(jnp.bfloat16)
    grad_pre = grad_pre.reshape(frame_count, channels)
    contract_first = (((0,), (0,)), ((), ()))
    tap_terms = [
        lax.dot_general(
            padded[k : k + frame_count],
            grad_pre,
            contract_first,
            preferred_element_type=jnp.float32,
        )
        for k in range(tap_count)
    ]
    seq_share = lax.psum_scatter(
        jnp.stack(tap_terms, axis=1), "seq", scatter_dimension=0, tiled=True
    )
    grad_weight = lax.psum_scatter(seq_share, "dp", scatter_dimension=2, tiled=True)
    return (merged[None], grad_weight)


def solution(mesh):
    in_specs = (
        P("dp", "seq", None),
        P("dp", "seq"),
        P(),
        P(),
        P("dp", None),
        P(),
        P("dp", "seq", None),
    )
    out_specs = (P("dp", "seq", None), P("seq", None, "dp"))
    return jax.shard_map(body, mesh=mesh, in_specs=in_specs, out_specs=out_specs, check_vma=False)
```

profile of v0, /device:TPU:2, one launch (start us, length us, event | category | flops | bytes accessed | tf_op | source)
XLA Modules:
  0.0 377.3 jit_solution(8471840743982743471)
XLA Ops:
  7.2 0.0 all-gather.2.cloned.1.call-start
  7.2 0.7 all-gather.2.cloned.1.call-update
  7.9 0.7 and_select_fusion
  8.6 0.1 fusion.22
  8.7 0.2 reduce_window_sum.11
  8.8 0.2 select_reduce_fusion
  9.0 0.7 fusion.23
  9.7 1.0 scatter_custom_fusion
  10.7 0.1 all_to_all.12
  10.8 22.3 %all_to_all.19 = s32[64,1,4]{2,1,0:T(1,128)S(1)} all-to-all(s32[64,1,4]{2,1,0:T(1,128)S(1)} %bitcast.73), channel_id=1, replica_groups=mesh['dp'=8,'seq'=64] {'seq'}, dimensions={0} | all-to-all | bytes 2048 | tf_op jit(solution)/shard_map/all_to_all | solution.py:60
  33.1 0.1 reshape.178
  33.2 1.4 gather_fusion
  34.5 1.2 reshape.174
  35.8 5.7 %all-to-all-start.2 = ((bf16[64,4,2048]{2,1,0:T(4,128)(2,1)}), bf16[64,4,2048]{2,1,0:T(4,128)(2,1)S(1)}, u32[]{:S(2)}, u32[]{:S(2)}) async-start(bf16[64,4,2048]{2,1,0:T(4,128)(2,1)} %reshape.174), calls=%async_computation.2 | async-start | bytes 2097152 | tf_op jit(solution)/shard_map/all_to_all | solution.py:69
  41.5 28.8 %all-to-all-done.2 = bf16[64,4,2048]{2,1,0:T(4,128)(2,1)S(1)} async-done(((bf16[64,4,2048]{2,1,0:T(4,128)(2,1)}), bf16[64,4,2048]{2,1,0:T(4,128)(2,1)S(1)}, u32[]{:S(2)}, u32[]{:S(2)}) %all-to-all-start.2) | async-done | bytes 1048608 | tf_op jit(solution)/shard_map/all_to_all | solution.py:69
  70.4 0.3 reshape.175
  70.6 0.9 gather_fusion.1
  71.6 10.2 %all-gather.2.cloned.1.call-done = bf16[1280,2048]{1,0:T(8,128)(2,1)} async-done(((bf16[160,2048]{1,0:T(8,128)(2,1)}), bf16[1280,2048]{1,0:T(8,128)(2,1)}) %all-gather.2.cloned.1.call-update) | async-done | bytes 5242896 | tf_op jit(solution)/shard_map/all_gather | solution.py:35
  81.7 4.3 %fusion.2 = f32[128,1280]{1,0:T(8,128)S(1)} fusion(bf16[128,2048]{1,0:T(8,128)(2,1)S(1)} %gather_fusion.1, bf16[1280,2048]{1,0:T(8,128)(2,1)} %all-gather.2.cloned.1.call-done), kind=kOutput, calls=%fused_computation.13 | convolution fusion | flops 671580160 | bytes 6422528 | tf_op jit(solution)/shard_map/dot_general | solution.py:71
  86.1 0.5 mul.82
  86.5 2.0 mul.83
  88.6 3.6 fusion.7
  92.1 2.1 reshape.171
  94.2 1.0 fusion.29
  95.2 4.2 %fusion = bf16[128,2048]{1,0:T(8,128)(2,1)} fusion(bf16[1280,2048]{1,0:T(8,128)(2,1)} %all-gather.2.cloned.1.call-done, f32[2048]{0:T(1024)S(1)} %copy-done.2, f32[128,1,1280]{2,1,0:T(1,128)S(1)} %get-tuple-element.5, f32[128,1,1280]{2,1,0:T(1,128)S(1)} %get-tuple-element.4), kind=kOutput, calls=%fused_computation.10 | convolution fusion | flops 672104448 | bytes 7086080 | tf_op jit(solution)/shard_map/dot_general | solution.py:50
  99.4 2.4 scatter_custom_fusion.1
  101.8 1.2 reshape.172
  103.1 10.9 %all-to-all-start.1 = ((bf16[64,4,2048]{2,1,0:T(4,128)(2,1)}), bf16[64,4,2048]{2,1,0:T(4,128)(2,1)S(1)}, u32[]{:S(2)}, u32[]{:S(2)}) async-start(bf16[64,4,2048]{2,1,0:T(4,128)(2,1)} %reshape.172), calls=%async_computation.1 | async-start | bytes 2097152 | tf_op jit(solution)/shard_map/all_to_all | solution.py:59
  114.0 0.0 all-reduce.4.cloned.1.call-start
  114.0 0.3 convolution_bitcast_fusion
  114.3 0.3 convolution_bitcast_fusion.2
  114.6 0.3 convolution_bitcast_fusion.1
  114.9 1.4 pad_maximum_fusion
  116.3 0.0 reduce-scatter.5.cloned.1.call-start
  116.4 1.3 dynamic-slice
  118.3 0.5 broadcast.196
  118.8 0.7 reduce.5
  119.6 0.1 reshape.169
  119.7 199.2 %all-reduce.4.cloned.1.call-done = f32[128,3,1280]{2,0,1:T(8,128)} async-done(((f32[128,3,1280]{2,0,1:T(8,128)}), f32[128,3,1280]{2,0,1:T(8,128)}) %all-reduce.4.cloned.1.call-update) | async-done | bytes 1966096
  318.8 0.9 constant_dynamic-slice_fusion
  319.8 2.0 copy.20
  321.8 3.8 reshape.219
  325.5 0.0 reduce-scatter.5.cloned.1.call-update
  325.5 38.5 %reduce-scatter.5.cloned.1.call-done = f32[160,6]{1,0:T(8,128)} async-done(((f32[1280,6]{1,0:T(8,128)}), f32[160,6]{1,0:T(8,128)}) %reduce-scatter.5.cloned.1.call-update) | async-done | bytes 3856
  364.0 1.1 reshape.220
  365.1 0.8 copy.21
  365.8 1.1 reshape.212
  366.9 3.8 %scatter_custom_fusion.2 = bf16[256,2048]{1,0:T(8,128)(2,1)} fusion(s32[256]{0:T(256)S(1)} %bitcast.74, bf16[256,2048]{1,0:T(8,128)(2,1)} %reshape.212, bf16[]{:T(256)} %constant.25.clone.1), kind=kCustom, calls=%fused_computation.26 | custom fusion | bytes 1049088 | tf_op jit(solution)/shard_map/scatter | solution.py:66
  (14 shorter events, 0.1 us)
Async XLA Ops:
  7.2 26.0 %copy-start = (bf16[1,256,2048]{2,1,0:T(8,128)(2,1)S(1)}, bf16[1,256,2048]{2,1,0:T(8,128)(2,1)}, u32[]{:S(2)}) copy-start(bf16[1,256,2048]{2,1,0:T(8,128)(2,1)} %param.13) | copy-start | bytes 3145732
  7.2 74.5 %all-gather.2.cloned.1.call-start = ((), (), s32[]{:S(2)}) async-start(), calls=%async_computation.4 | async-start | bytes 5898240 | tf_op jit(solution)/shard_map/all_gather | solution.py:35
  35.8 5.7 %copy-start.1 = (bf16[1,256,128]{2,1,0:T(8,128)(2,1)S(1)}, bf16[1,256,128]{2,1,0:T(8,128)(2,1)}, u32[]{:S(2)}) copy-start(bf16[1,256,128]{2,1,0:T(8,128)(2,1)} %param.7) | copy-start | bytes 196612
  35.8 34.6 %all-to-all-start.2 = ((bf16[64,4,2048]{2,1,0:T(4,128)(2,1)}), bf16[64,4,2048]{2,1,0:T(4,128)(2,1)S(1)}, u32[]{:S(2)}, u32[]{:S(2)}) async-start(bf16[64,4,2048]{2,1,0:T(4,128)(2,1)} %reshape.174), calls=%async_computation.2 | async-start | bytes 2097152 | tf_op jit(solution)/shard_map/all_to_all | solution.py:69
  86.5 2.0 copy-start.3
  94.2 1.0 copy-start.2
  103.1 262.8 %all-to-all-start.1 = ((bf16[64,4,2048]{2,1,0:T(4,128)(2,1)}), bf16[64,4,2048]{2,1,0:T(4,128)(2,1)S(1)}, u32[]{:S(2)}, u32[]{:S(2)}) async-start(bf16[64,4,2048]{2,1,0:T(4,128)(2,1)} %reshape.172), calls=%async_computation.1 | async-start | bytes 2097152 | tf_op jit(solution)/shard_map/all_to_all | solution.py:59
  114.0 204.9 %all-reduce.4.cloned.1.call-start = ((), (), s32[]{:S(2)}) async-start(), calls=%async_computation.6 | async-start | bytes 3932160
  116.3 247.7 %reduce-scatter.5.cloned.1.call-start = ((), (), s32[]{:S(2)}) async-start(), calls=%async_computation.5 | async-start | bytes 737280
Sparse Core Ops, SparseCore 0:
  10.1 71.5 all-gather.1
  118.2 200.5 all-reduce.3
  325.7 38.3 reduce-scatter.4
where the time goes:
time: 378 us; the launch traced here: 377 us
  waiting for transfers between devices  277 us (73%)
  local copies, waits for them, and re-layouts  29.4 us (8%)
  blocking collectives  22.3 us (6%)
  starting transfers between devices  16.7 us (4%)
  between operations  14.6 us (4%)
  matrix products  12.9 us (3%)
  other arithmetic  3.93 us (1%)
    unnamed x5, waiting for transfers between devices  238 us
    all_to_all x1, waiting for transfers between devices, body(): lax.all_to_all(picked, 'seq', split_axis=0, concat_axis=0, tiled=True)  28.8 us
    all_to_all x1, blocking collectives, body(): lax.all_to_all(dest_rows, 'seq', split_axis=0, concat_axis=0, tiled=True)  22.3 us
    all_to_all x1, starting transfers between devices, body(): lax.all_to_all(outgoing, 'seq', split_axis=0, concat_axis=0, tiled=True)  10.9 us
    all_gather x1, waiting for transfers between devices, body(): full_weight = lax.all_gather(proj_weight, 'dp', axis=0, tiled=True)  10.2 us
    unnamed x14, local copies, waits for them, and re-layouts  9.77 us
  transfers between devices with their start and end apart: 5, of which 4 were waited for; matrix products, arithmetic and copies ran while one was open for 5% of the time, Pallas kernels for 0%

commit v1 on v0

--- a/solution.py
+++ b/solution.py
@@ -32,7 +32,15 @@
     pre_act = jnp.dot(stacked, kernel, preferred_element_type=jnp.float32) + conv_bias
     act_pairs = gelu_value(pre_act).reshape(tok_count, 2, channels)
     pooled = (0.5 * (act_pairs[:, 0, :] + act_pairs[:, 1, :])).astype(jnp.bfloat16)
-    full_weight = lax.all_gather(proj_weight, "dp", axis=0, tiled=True)
+    full_weight = jnp.concatenate(
+        jax.lax.all_to_all(
+            jnp.stack([proj_weight] * jax.lax.axis_size("dp")),
+            concat_axis=0,
+            split_axis=0,
+            axis_name="dp",
+        ),
+        axis=0,
+    )
     owner_index = local_spots // rows_own
     owner_row = local_spots % rows_own
     onehot = (owner_index[:, None] == jnp.arange(owner_count, dtype=jnp.int32)[None, :]).astype(

time: 378 us -> 487 us (1.29)
  waiting for transfers between devices: 277 us -> 352 us
  blocking collectives: 22.3 us -> 56.9 us
    all_to_all x1, waiting for transfers between devices: 28.8 us -> 117 us  [body(): jax.lax.all_to_all(jnp.stack([proj_weight] * jax.lax.axis_size('dp')), co...]
    all_to_all x0 -> x1, blocking collectives: none -> 34.6 us  [body(): lax.all_to_all(picked, 'seq', split_axis=0, concat_axis=0, tiled=True)]
    all_gather x1 -> x0, waiting for transfers between devices: 10.2 us -> none  [body(): full_weight = lax.all_gather(proj_weight, 'dp', axis=0, tiled=True)]
    unnamed x5 -> x4, waiting for transfers between devices: 238 us -> 235 us
    unnamed x14 -> x16, local copies, waits for them, and re-layouts: 9.77 us -> 9.77 us
  transfers between devices with their start and end apart: 5 -> 4, of which waited for: 4 -> 3; matrix products, arithmetic and copies ran while one was open for 5% -> 3% of each run, Pallas kernels for 0% -> 0%
where the time goes in v1:
time: 487 us
  waiting for transfers between devices  352 us (72%)
  blocking collectives  56.9 us (12%)
  local copies, waits for them, and re-layouts  32.3 us (7%)
  between operations  14.9 us (3%)
  starting transfers between devices  13.9 us (3%)
  matrix products  12.9 us (3%)
    unnamed x4, waiting for transfers between devices  235 us
    all_to_all x1, waiting for transfers between devices, body(): jax.lax.all_to_all(jnp.stack([proj_weight] * jax.lax.axis_size('dp')), co...  117 us
    all_to_all x1, blocking collectives, body(): lax.all_to_all(picked, 'seq', split_axis=0, concat_axis=0, tiled=True)  34.6 us
    all_to_all x1, blocking collectives, body(): lax.all_to_all(dest_rows, 'seq', split_axis=0, concat_axis=0, tiled=True)  22.3 us
    unnamed x16, local copies, waits for them, and re-layouts  9.77 us
  transfers between devices with their start and end apart: 4, of which 3 were waited for; matrix products, arithmetic and copies ran while one was open for 3% of the time, Pallas kernels for 0%

profile of v1, /device:TPU:2, one launch (start us, length us, event | category | flops | bytes accessed | tf_op | source)
XLA Modules:
  0.0 486.5 jit_solution(15610738796494832421)
XLA Ops:
  7.2 0.8 and_select_fusion
  7.9 0.1 fusion.22
  8.0 0.2 reduce_window_sum.11
  8.2 0.2 select_reduce_fusion
  8.4 0.7 fusion.23
  9.0 1.0 scatter_custom_fusion
  10.0 0.1 all_to_all.15
  10.1 22.3 %all_to_all.24 = s32[64,1,4]{2,1,0:T(1,128)S(1)} all-to-all(s32[64,1,4]{2,1,0:T(1,128)S(1)} %bitcast.74), channel_id=1, replica_groups=mesh['dp'=8,'seq'=64] {'seq'}, dimensions={0} | all-to-all | bytes 2048 | tf_op jit(solution)/shard_map/all_to_all | solution.py:68
  32.4 0.1 reshape.181
  32.5 1.4 gather_fusion
  33.9 1.2 reshape.177
  35.1 34.6 %all_to_all.25 = bf16[64,4,2048]{2,1,0:T(4,128)(2,1)S(1)} all-to-all(bf16[64,4,2048]{2,1,0:T(4,128)(2,1)} %reshape.177), channel_id=1, replica_groups=mesh['dp'=8,'seq'=64] {'seq'}, dimensions={0} | all-to-all | bytes 2097152 | tf_op jit(solution)/shard_map/all_to_all | solution.py:77
  69.8 3.0 stack.10
  72.8 7.2 %all-to-all-start.1 = ((bf16[8,160,2048]{2,1,0:T(8,128)(2,1)}), bf16[8,160,2048]{2,1,0:T(8,128)(2,1)}, u32[]{:S(2)}, u32[]{:S(2)}) async-start(bf16[8,160,2048]{2,1,0:T(8,128)(2,1)} %stack.10), calls=%async_computation.1 | async-start | bytes 10485760 | tf_op jit(solution)/shard_map/all_to_all | solution.py:36
  80.1 0.3 reshape.178
  80.3 0.9 gather_fusion.1
  81.3 116.6 %all-to-all-done.1 = bf16[8,160,2048]{2,1,0:T(8,128)(2,1)} async-done(((bf16[8,160,2048]{2,1,0:T(8,128)(2,1)}), bf16[8,160,2048]{2,1,0:T(8,128)(2,1)}, u32[]{:S(2)}, u32[]{:S(2)}) %all-to-all-start.1) | async-done | bytes 5242912 | tf_op jit(solution)/shard_map/all_to_all | solution.py:36
  197.9 4.3 fusion.2
  202.3 0.5 mul.82
  202.8 2.0 mul.83
  204.8 3.5 fusion.7
  208.3 2.1 reshape.173
  210.4 1.0 fusion.29
  211.4 4.2 fusion
  215.6 2.2 scatter_custom_fusion.1
  217.8 1.2 reshape.175
  219.0 6.4 %all-to-all-start.2 = ((bf16[64,4,2048]{2,1,0:T(4,128)(2,1)}), bf16[64,4,2048]{2,1,0:T(4,128)(2,1)S(1)}, u32[]{:S(2)}, u32[]{:S(2)}) async-start(bf16[64,4,2048]{2,1,0:T(4,128)(2,1)} %reshape.175), calls=%async_computation.2 | async-start | bytes 2097152 | tf_op jit(solution)/shard_map/all_to_all | solution.py:67
  225.4 0.0 all-reduce.4.cloned.1.call-start
  225.5 0.3 convolution_bitcast_fusion
  225.8 0.3 convolution_bitcast_fusion.2
  226.1 0.3 convolution_bitcast_fusion.1
  226.4 1.4 pad_maximum_fusion
  227.8 0.0 all-reduce.4.cloned.1.call-update
  227.8 0.3 reduce-scatter.5.cloned.1.call-start
  228.1 1.3 dynamic-slice
  230.0 0.5 broadcast.197
  230.5 0.7 reduce.5
  231.3 0.1 reshape.171
  231.4 196.4 %all-reduce.4.cloned.1.call-done = f32[128,3,1280]{2,0,1:T(8,128)} async-done(((f32[128,3,1280]{2,0,1:T(8,128)}), f32[128,3,1280]{2,0,1:T(8,128)}) %all-reduce.4.cloned.1.call-update) | async-done | bytes 1966096
  427.8 0.9 constant_dynamic-slice_fusion
  428.7 2.0 copy.20
  430.7 3.8 reshape.222
  434.4 0.0 reduce-scatter.5.cloned.1.call-update
  434.5 38.5 %reduce-scatter.5.cloned.1.call-done = f32[160,6]{1,0:T(8,128)} async-done(((f32[1280,6]{1,0:T(8,128)}), f32[160,6]{1,0:T(8,128)}) %reduce-scatter.5.cloned.1.call-update) | async-done | bytes 3856
  472.9 1.1 reshape.223
  474.0 0.8 copy.21
  474.7 1.1 reshape.215
  475.9 3.8 scatter_custom_fusion.2
  (15 shorter events, 0.1 us)
Async XLA Ops:
  7.2 25.4 %copy-start = (bf16[1,256,2048]{2,1,0:T(8,128)(2,1)S(1)}, bf16[1,256,2048]{2,1,0:T(8,128)(2,1)}, u32[]{:S(2)}) copy-start(bf16[1,256,2048]{2,1,0:T(8,128)(2,1)} %param.13) | copy-start | bytes 3145732
  35.1 34.6 %copy-start.2 = (bf16[160,2048]{1,0:T(8,128)(2,1)S(1)}, bf16[160,2048]{1,0:T(8,128)(2,1)}, u32[]{:S(2)}) copy-start(bf16[160,2048]{1,0:T(8,128)(2,1)} %param.11) | copy-start | bytes 1966084
  72.8 7.2 %copy-start.1 = (bf16[1,256,128]{2,1,0:T(8,128)(2,1)S(1)}, bf16[1,256,128]{2,1,0:T(8,128)(2,1)}, u32[]{:S(2)}) copy-start(bf16[1,256,128]{2,1,0:T(8,128)(2,1)} %param.7) | copy-start | bytes 196612
  72.8 125.2 %all-to-all-start.1 = ((bf16[8,160,2048]{2,1,0:T(8,128)(2,1)}), bf16[8,160,2048]{2,1,0:T(8,128)(2,1)}, u32[]{:S(2)}, u32[]{:S(2)}) async-start(bf16[8,160,2048]{2,1,0:T(8,128)(2,1)} %stack.10), calls=%async_computation.1 | async-start | bytes 10485760 | tf_op jit(solution)/shard_map/all_to_all | solution.py:36
  202.7 2.0 copy-start.4
  210.4 1.0 copy-start.3
  219.0 255.7 %all-to-all-start.2 = ((bf16[64,4,2048]{2,1,0:T(4,128)(2,1)}), bf16[64,4,2048]{2,1,0:T(4,128)(2,1)S(1)}, u32[]{:S(2)}, u32[]{:S(2)}) async-start(bf16[64,4,2048]{2,1,0:T(4,128)(2,1)} %reshape.175), calls=%async_computation.2 | async-start | bytes 2097152 | tf_op jit(solution)/shard_map/all_to_all | solution.py:67
  225.4 202.3 %all-reduce.4.cloned.1.call-start = ((), (), s32[]{:S(2)}) async-start(), calls=%async_computation.6 | async-start | bytes 3932160
  227.8 245.1 %reduce-scatter.5.cloned.1.call-start = ((), (), s32[]{:S(2)}) async-start(), calls=%async_computation.5 | async-start | bytes 737280
Sparse Core Ops, SparseCore 0:
  229.7 197.9 all-reduce.3
  434.6 38.3 reduce-scatter.4
